TPU v7x, 128 devices: a whole 4x4x4 slice. The times are simulated.
128 devices in a mesh: req: 4 (over y), seq: 32 (over x, z, core).
Axes of the slice: x: 4, y: 4, z: 4, core: 2. Of those that a mesh axis runs over, the one named last changes fastest.
Arguments:
- tokens: bfloat16 [4, 4096, 2048], P('req', 'seq'), may hold values from -6 to 6
- lengths: int32 [4, 4], replicated, may hold values from 1 to 2048, as said below
- attn_gain: bfloat16 [2048], replicated, may hold values from 0.099609375 to 1.8984375
- w_query: bfloat16 [2048, 512], replicated, may hold values from -0.125 to 0.125
- w_key: bfloat16 [2048, 512], replicated, may hold values from -0.125 to 0.125
- w_value: bfloat16 [2048, 1024], replicated, may hold values from -0.125 to 0.125
- w_outgate: bfloat16 [2048, 1024], replicated, may hold values from -0.125 to 0.125
- gate_down: bfloat16 [2048, 16], replicated, may hold values from -1 to 1
- gate_up: bfloat16 [16, 512], replicated, may hold values from -2 to 2
- gate_bias: float32 [512], replicated, may hold values from -1 to 8
- conv_weight: bfloat16 [4, 2048], replicated, may hold values from -2 to 2
- head_gain: bfloat16 [512], replicated, may hold values from 0.099609375 to 1.8984375
- w_out: bfloat16 [1024, 2048], replicated, may hold values from -0.1875 to 0.1875
- forward_norm_scale: bfloat16 [2048], replicated, may hold values from 0.099609375 to 1.8984375
- w_gate: bfloat16 [2048, 2816], P('seq', 'req'), may hold values from -0.125 to 0.125
- w_up: bfloat16 [2048, 2816], P('seq', 'req'), may hold values from -0.125 to 0.125
- down_weight: bfloat16 [2048, 2816], P('seq', 'req'), may hold values from -0.109375 to 0.109375
Outputs:
- output: bfloat16 [4, 4096, 2048], P('req', 'seq')
Inputs may be any that keep to these rules, and one draw needn't show every extreme that they name: Row g lists the prompt lengths of group g's 4 requests, packed in slot order from position 0 of the group; every row holds one length equal to 2048; rows 2i and 2i + 1 together sum to 6144, so all rows sum to 12288; each row sums to between 2052 and 4092.
All inputs are finite; a program needn't handle non-finite values.
Results may differ from a plain program's by a relative error of at most 0.008.
Values may be sent and summed in bfloat16 or wider, within the bound.
A program may use at most 128 MiB of HBM per device.

v0:
```python
import jax
import jax.numpy as jnp
from jax import lax
from jax.sharding import PartitionSpec as P

HEADS = 2
SPAN = 64
EPSILON = 1e-05
NORMALIZER = 16.0
MAXIMUM_ACCURACY = lax.Precision.HIGHEST


def prefix_2(shard, axis, combine, identity):
    size, mine = (lax.axis_size(axis), lax.axis_index(axis))
    everything = jax.tree.map(lambda part: lax.all_gather(part, axis), shard)
    start = jax.tree.map(
        lambda part, zero: jnp.broadcast_to(jnp.asarray(zero, part.dtype), part.shape),
        shard,
        identity,
    )

    def lap(k, before):
        reached = k < mine
        new = combine(before, jax.tree.map(lambda part: part[k], everything))
        return jax.tree.map(lambda a, b: jnp.where(reached, a, b), new, before)

    return lax.fori_loop(0, size, lap, start)


def from_behind(value, axis, steps):
    count = lax.axis_size(axis)
    initial, last = (max(0, -steps), min(count, count - steps))
    return lax.ppermute(value, axis, [(source, source + steps) for source in range(initial, last)])


def rms_scale(values, gain):
    mean_square = jnp.mean(values * values, axis=-1, keepdims=True)
    return values * lax.rsqrt(mean_square + EPSILON) * gain


def segment_ids(positions, bounds):
    return jnp.sum((positions[:, None] >= bounds[None, :]).astype(jnp.int32), axis=1)


def pick_group(table, indices):
    match = indices[:, None] == jnp.arange(table.shape[0], dtype=jnp.int32)[None, :]
    return jnp.sum(jnp.where(match, table[None, :], 0), axis=1)


def short_conv(extended, segment_ext, conv_weight, count):
    taps = conv_weight.shape[0]
    own_segment = segment_ext[taps - 1 :]
    total = jnp.zeros((count, extended.shape[1]), jnp.float32)
    for tap_index in range(taps):
        first = taps - 1 - tap_index
        shifted = extended[first : first + count].astype(jnp.float32)
        same = (segment_ext[first : first + count] == own_segment).astype(jnp.float32)
        total = total + conv_weight[tap_index].astype(jnp.float32) * shifted * same[:, None]
    return total


def span_cumulative(log_decay):
    span_len, head_count, key_width = log_decay.shape
    lower = jnp.tril(jnp.ones((span_len, span_len), jnp.float32))
    flat = jnp.dot(
        lower, log_decay.reshape(span_len, head_count * key_width), precision=MAXIMUM_ACCURACY
    )
    return flat.reshape(span_len, head_count, key_width)


def state_update(
    recurrent_state, cumulative, keys_float, value_rows_wide, segment_span, clean_last
):
    tail = cumulative[-1]
    keep = (segment_span == segment_span[-1]).astype(jnp.float32)
    weighted_values = keys_float * jnp.exp(tail[None] - cumulative) * keep[:, None, None]
    state_increment = jnp.einsum(
        "ugl,ugi->gli", weighted_values, value_rows_wide, precision=MAXIMUM_ACCURACY
    )
    return recurrent_state * (jnp.exp(tail) * clean_last)[:, :, None] + state_increment


def span_state(recurrent_state, items):
    query, keys, values, log_decay, segment_span, segment_before = items
    cumulative = span_cumulative(log_decay)
    clean_last = (segment_span[-1] == segment_before).astype(jnp.float32)
    new_state = state_update(
        recurrent_state,
        cumulative,
        keys.astype(jnp.float32),
        values.astype(jnp.float32),
        segment_span,
        clean_last,
    )
    return (new_state, None)


def span_attend(recurrent_state, items):
    query, keys, values, log_decay, segment_span, segment_before = items
    cumulative = span_cumulative(log_decay)
    query_float = query.astype(jnp.float32)
    keys_float = keys.astype(jnp.float32)
    clean = (segment_span == segment_before).astype(jnp.float32)
    query_decayed_rows = query_float * jnp.exp(cumulative) * clean[:, None, None]
    carried_forward = jnp.einsum(
        "ynj,njc->ync", query_decayed_rows, recurrent_state, precision=MAXIMUM_ACCURACY
    )
    order = jnp.arange(segment_span.shape[0])
    allowed = (segment_span[:, None] == segment_span[None, :]) & (order[:, None] >= order[None, :])
    gap = jnp.where(allowed[:, :, None, None], cumulative[:, None] - cumulative[None, :], 0.0)
    scores = jnp.sum(query_float[:, None] * keys_float[None, :] * jnp.exp(gap), axis=-1)
    scores = scores * allowed[:, :, None].astype(jnp.float32)
    inner = jnp.einsum(
        "tsh,shv->thv", scores.astype(jnp.bfloat16), values, preferred_element_type=jnp.float32
    )
    new_state = state_update(
        recurrent_state, cumulative, keys_float, values.astype(jnp.float32), segment_span, clean[-1]
    )
    return (new_state, (carried_forward + inner, cumulative))


def combine_states(earlier, later):
    return (earlier[0] * later[0], later[0][:, :, None] * earlier[1] + later[1])


def carry_in(decay_block, block_state):
    identity = (jnp.ones_like(decay_block), jnp.zeros_like(block_state))
    prefix = prefix_2((decay_block, block_state), "seq", combine_states, identity)
    return prefix[1]


def swiglu_rows(resident, forward_norm_scale, w_gate, w_up, down_weight):
    normed = rms_scale(resident.astype(jnp.float32), forward_norm_scale.astype(jnp.float32)).astype(
        jnp.bfloat16
    )
    every_row = lax.all_gather(normed, "req", axis=0, tiled=True)
    gate_full, up_full, down_full = (
        lax.all_gather(w_gate, "seq", axis=0, tiled=True),
        lax.all_gather(w_up, "seq", axis=0, tiled=True),
        lax.all_gather(down_weight, "seq", axis=0, tiled=True),
    )
    gate = jnp.dot(every_row, gate_full, preferred_element_type=jnp.float32)
    upward = jnp.dot(every_row, up_full, preferred_element_type=jnp.float32)
    hidden = (jax.nn.silu(gate) * upward).astype(jnp.bfloat16)
    summed = lax.psum_scatter(
        lax.dot_general(
            hidden, down_full, (((1,), (1,)), ((), ())), preferred_element_type=jnp.float32
        ),
        "req",
        scatter_dimension=0,
        tiled=True,
    )
    return summed.astype(jnp.bfloat16)


def shards(
    tokens,
    lengths,
    attn_gain,
    w_query,
    w_key,
    w_value,
    w_outgate,
    gate_down,
    gate_up,
    gate_bias,
    conv_weight,
    head_gain,
    w_out,
    forward_norm_scale,
    w_gate,
    w_up,
    down_weight,
):
    seq_count = lax.axis_size("seq")
    req_count = lax.axis_size("req")
    group_index = lax.axis_index("req")
    slice_index = lax.axis_index("seq")
    inputs = tokens[0]
    block_rows = inputs.shape[0]
    request_slots = lengths.shape[1]
    bounds_all = jnp.cumsum(lengths, axis=1)
    totals = bounds_all[:, -1]
    offsets = jnp.cumsum(totals) - totals
    group_row = jnp.arange(lengths.shape[0], dtype=jnp.int32) == group_index
    bounds = jnp.sum(jnp.where(group_row[:, None], bounds_all, 0), axis=0)
    start_pos = slice_index * block_rows
    positions = start_pos + jnp.arange(block_rows, dtype=jnp.int32)
    segment = segment_ids(positions, bounds)
    valid = segment < request_slots
    normed = rms_scale(inputs.astype(jnp.float32), attn_gain.astype(jnp.float32)).astype(
        jnp.bfloat16
    )
    projected = jnp.concatenate(
        [
            jnp.dot(normed, w_query, preferred_element_type=jnp.float32),
            jnp.dot(normed, w_key, preferred_element_type=jnp.float32),
            jnp.dot(normed, w_value, preferred_element_type=jnp.float32),
        ],
        axis=1,
    ).astype(jnp.bfloat16)
    outgate = jnp.dot(normed, w_outgate, preferred_element_type=jnp.float32)
    latent = jnp.dot(normed, gate_down, preferred_element_type=jnp.float32)
    logits = jnp.dot(latent, gate_up.astype(jnp.float32), precision=MAXIMUM_ACCURACY) + gate_bias
    log_decay = jax.nn.log_sigmoid(logits) / NORMALIZER
    taps = conv_weight.shape[0]
    edge_rows = projected[block_rows - (taps - 1) :]
    previous = from_behind(edge_rows, "seq", 1)
    extended = jnp.concatenate([previous, projected], axis=0)
    segment_ext = segment_ids(
        start_pos - (taps - 1) + jnp.arange(block_rows + taps - 1, dtype=jnp.int32), bounds
    )
    convolved = jax.nn.silu(short_conv(extended, segment_ext, conv_weight, block_rows)).astype(
        jnp.bfloat16
    )
    key_total = w_query.shape[1]
    value_total = w_value.shape[1]
    key_width = key_total // HEADS
    value_width = value_total // HEADS
    span_count = block_rows // SPAN
    query = convolved[:, :key_total].reshape(span_count, SPAN, HEADS, key_width)
    keys = convolved[:, key_total : 2 * key_total].reshape(span_count, SPAN, HEADS, key_width)
    values = convolved[:, 2 * key_total :].reshape(span_count, SPAN, HEADS, value_width)
    decay_spans = log_decay.reshape(span_count, SPAN, HEADS, key_width)
    segment_spans = segment.reshape(span_count, SPAN)
    segment_before = segment_ids(
        start_pos - 1 + SPAN * jnp.arange(span_count, dtype=jnp.int32), bounds
    )
    items = (query, keys, values, decay_spans, segment_spans, segment_before)
    block_clean = (segment[-1] == segment_before[0]).astype(jnp.float32)
    decay_block = jnp.exp(jnp.sum(log_decay, axis=0)).reshape(HEADS, key_width) * block_clean
    zero_state = jnp.zeros((HEADS, key_width, value_width), jnp.float32)
    block_state, unused = lax.scan(span_state, zero_state, items)
    incoming = carry_in(decay_block, block_state)
    final_state, (attended, cumulative) = lax.scan(span_attend, incoming, items)
    attended = attended.reshape(block_rows, HEADS, value_width)
    gated = rms_scale(attended, head_gain.astype(jnp.float32)).reshape(
        block_rows, value_total
    ) * jax.nn.silu(outgate)
    resident = (
        jnp.dot(gated.astype(jnp.bfloat16), w_out, preferred_element_type=jnp.float32)
        + inputs.astype(jnp.float32)
    ).astype(jnp.bfloat16)
    dev_count = req_count * seq_count
    own_index = group_index * seq_count + slice_index
    parallel_width = block_rows // dev_count
    capacity = 3 * block_rows // 4
    own_total = jnp.sum(jnp.where(group_row, totals, 0))
    own_offset = jnp.sum(jnp.where(group_row, offsets, 0))
    own_count = jnp.clip(own_total - start_pos, 0, block_rows)
    own_phase = (own_offset + start_pos) % dev_count
    target_slots = jnp.arange(dev_count, dtype=jnp.int32)[:, None]
    lanes = jnp.arange(parallel_width, dtype=jnp.int32)[None, :]
    source_rows = (target_slots - own_phase) % dev_count + lanes * dev_count
    outgoing = jnp.take(resident, source_rows.reshape(-1), axis=0).reshape(
        dev_count, parallel_width, -1
    )
    outgoing = jnp.where((source_rows < own_count)[:, :, None], outgoing, 0)
    arrived = lax.all_to_all(
        outgoing, ("req", "seq"), split_axis=0, concat_axis=0, tiled=True
    ).reshape(dev_count * parallel_width, -1)
    ranks = jnp.arange(capacity, dtype=jnp.int32) * dev_count + own_index
    owner = jnp.sum((ranks[:, None] >= offsets[None, :]).astype(jnp.int32), axis=1) - 1
    owner_offset = pick_group(offsets, owner)
    within = ranks - owner_offset
    owner_slice = within // block_rows
    owner_phase = (owner_offset + owner_slice * block_rows) % dev_count
    owner_lane = (owner_phase + within % block_rows) // dev_count - (
        own_index < owner_phase
    ).astype(jnp.int32)
    gathered = jnp.take(
        arrived, (owner * seq_count + owner_slice) * parallel_width + owner_lane, axis=0
    )
    processed = swiglu_rows(gathered, forward_norm_scale, w_gate, w_up, down_weight)
    senders = jnp.arange(dev_count, dtype=jnp.int32)
    sender_group = senders // seq_count
    sender_slice = senders % seq_count
    sender_base = pick_group(offsets, sender_group) + sender_slice * block_rows
    sender_phase = sender_base % dev_count
    sender_rows = (own_index - sender_phase[:, None]) % dev_count + lanes * dev_count
    sender_count = jnp.clip(
        pick_group(totals, sender_group) - sender_slice * block_rows, 0, block_rows
    )
    home_slot = jnp.clip((sender_base[:, None] + sender_rows) // dev_count, 0, capacity - 1)
    returning = jnp.take(processed, home_slot.reshape(-1), axis=0).reshape(
        dev_count, parallel_width, -1
    )
    returning = jnp.where((sender_rows < sender_count[:, None])[:, :, None], returning, 0)
    returned = lax.all_to_all(
        returning, ("req", "seq"), split_axis=0, concat_axis=0, tiled=True
    ).reshape(dev_count * parallel_width, -1)
    device_local_rows = jnp.arange(block_rows, dtype=jnp.int32)
    target_of = (own_phase + device_local_rows) % dev_count
    lane_of = (own_phase + device_local_rows) // dev_count - (target_of < own_phase).astype(
        jnp.int32
    )
    mlp_own = jnp.take(
        returned,
        jnp.clip(target_of * parallel_width + lane_of, 0, dev_count * parallel_width - 1),
        axis=0,
    )
    output = jnp.where(
        valid[:, None], resident.astype(jnp.float32) + mlp_own.astype(jnp.float32), 0.0
    ).astype(jnp.bfloat16)
    return output[None]


def solution(mesh):
    return jax.shard_map(
        shards,
        mesh=mesh,
        in_specs=(
            P("req", "seq", None),
            P(),
            P(),
            P(),
            P(),
            P(),
            P(),
            P(),
            P(),
            P(),
            P(),
            P(),
            P(),
            P(),
            P("seq", "req"),
            P("seq", "req"),
            P("seq", "req"),
        ),
        out_specs=P("req", "seq", None),
        check_vma=False,
    )
```

profile of v0, /device:TPU:1, one launch (start us, length us, event | category | flops | bytes accessed | tf_op | source)
XLA Modules:
  0.0 449.4 jit_solution(5662476398953703670)
XLA Ops:
  7.4 1.2 fusion.56
  8.6 3.3 convolution_convert_fusion
  13.1 4.9 %collective-permute-start = (bf16[3,2048]{1,0:T(4,128)(2,1)S(1)}, bf16[3,2048]{1,0:T(4,128)(2,1)S(1)}, u32[]{:S(2)}, u32[]{:S(2)}) collective-permute-start(bf16[3,2048]{1,0:T(4,128)(2,1)S(1)} %slice.105), channel_id=1, source_target_pairs={{0,1},{1,2},{2,3},{3,4},{4,5},{5,6},{6,7},{7,8},{8,9},{9,10},{10,1... | collective-permute-start | bytes 36872 | tf_op jit(solution)/shard_map/ppermute | solution.py:33
  21.2 9.2 %while.38 = (s32[]{:T(128)}, f32[2,256,512]{2,1,0:T(8,128)S(1)}, f32[2,64,2,256]{3,2,1,0:T(2,128)S(1)}, s32[2,64]{1,0:T(2,128)S(1)}, s32[2]{0:T(128)S(1)}, /*ind...) while((s32[]{:T(128)}, f32[2,256,512]{2,1,0:T(8,128)S(1)}, ...), condition=%wide.region_8.9_spmd.clone, body=%wide.region_7.8_spmd.clone.sunk | while | flops 227418752 | bytes 3230365 | solution.py:233
  30.4 1.0 copy-done.2
  35.1 26.4 %all_gather.22 = f32[32,2,256]{2,1,0:T(2,128)S(1)} all-gather(f32[1,2,256]{2,1,0:T(2,128)S(1)} %mul.395), channel_id=1, replica_groups=mesh['req'=4,'seq'=32] {'seq'}, dimensions={0}, use_global_device_ids=true | all-gather | bytes 67584 | tf_op jit(solution)/shard_map/all_gather | solution.py:15
  62.5 84.9 %all-gather.15.cloned.1.call-done = f32[64,256,512]{2,1,0:T(8,128)} async-done(((f32[2,256,512]{2,1,0:T(8,128)}), f32[64,256,512]{2,1,0:T(8,128)}) %all-gather.15.cloned.1.call-update) | async-done | bytes 33554448 | tf_op jit(solution)/shard_map/all_gather | solution.py:15
  147.4 49.0 %while.39 = (s32[]{:T(128)}, f32[2,256,512]{2,1,0:T(8,128)S(1)}, s32[]{:T(128)}, f32[32,2,256]{2,1,0:T(2,128)S(1)}, f32[32,2,256,512]{3,2,1,0:T(8,128)}, /*index=5*/s32[]{:T(128)}, s32[]{:T(128)}) while((s32[]{:T(128)}, f32[2,256,512]{2,1,0:T(8,128)S(1)}, s32[]{:T(128)}, f32[32,2,256]{2,1,0:T(2,128)S(1)}, ...), condition=%wide.region_10.11_spmd.clone, body=%wide.region_9.10_spmd.clone.sunk | while | flops 1048580 | bytes 3151977 | solution.py:27
  147.4 1.5 fusion.165
  149.0 1.5 fusion.165
  150.5 1.5 fusion.165
  152.0 1.5 fusion.165
  153.6 1.5 fusion.165
  155.1 1.5 fusion.165
  156.6 1.5 fusion.165
  158.1 1.5 fusion.165
  159.7 1.5 fusion.165
  161.2 1.5 fusion.165
  162.7 1.5 fusion.165
  164.3 1.5 fusion.165
  165.8 1.5 fusion.165
  167.3 1.5 fusion.165
  168.9 1.5 fusion.165
  170.4 1.5 fusion.165
  171.9 1.5 fusion.165
  173.4 1.5 fusion.165
  175.0 1.5 fusion.165
  176.5 1.5 fusion.165
  178.0 1.5 fusion.165
  179.6 1.5 fusion.165
  181.1 1.5 fusion.165
  182.7 1.5 fusion.165
  184.2 1.5 fusion.165
  185.8 1.5 fusion.165
  187.3 1.5 fusion.165
  188.8 1.5 fusion.165
  190.4 1.5 fusion.165
  191.9 1.5 fusion.165
  193.4 1.5 fusion.165
  195.0 1.5 fusion.165
  196.5 19.7 %while.37 = (s32[]{:T(128)}, f32[2,256,512]{2,1,0:T(8,128)S(1)}, f32[2,64,2,512]{3,1,2,0:T(8,128)S(1)}, f32[2,64,2,256]{3,2,1,0:T(2,128)S(1)}, s32[2,64]{1,0:T(2...) while((s32[]{:T(128)}, f32[2,256,512]{2,1,0:T(8,128)S(1)}, ...), condition=%wide.region_13.14_spmd, body=%wide.region_11.13_spmd.sunk | while | flops 447611648 | bytes 7385501 | solution.py:235
  198.6 3.0 multiply_reduce_fusion.3
  205.3 1.0 convolution_add_fusion.6
  208.4 3.0 multiply_reduce_fusion.3
  215.1 1.0 convolution_add_fusion.6
  217.2 4.9 %fusion.53 = bf16[128,2048]{1,0:T(8,128)(2,1)S(1)} fusion(bf16[1024,2048]{1,0:T(8,128)(2,1)} %param.37, bf16[1,128,2048]{2,1,0:T(8,128)(2,1)S(1)} %copy-done.3, f32[128,1024]{1,0:T(8,128)S(1)} %bitcast.254, f32[128,1024]{1,0:T(8,128)S(1)} %bitcast.253, f32[1024]{0:T(1024)S(1)} %bitcast.261, bf16[2048,1024]{1,0:T(8,128)(2,1)} %param.31, ...), kind=kOutput, calls=%fused_computation.82 | convolution fusion | flops 1076625408 | bytes 10498560 | tf_op jit(solution)/shard_map/dot_general | solution.py:241
  223.8 1.0 reduce.12
  224.9 1.2 reshape.936
  226.0 7.1 %all-to-all-start = ((bf16[128,2,1024]{2,1,0:T(2,128)(2,1)}), bf16[128,2,1024]{2,1,0:T(2,128)(2,1)S(1)}, u32[]{:S(2)}, u32[]{:S(2)}) async-start(bf16[128,2,1024]{2,1,0:T(2,128)(2,1)} %reshape.936), calls=%async_computation | async-start | bytes 1048576 | tf_op jit(solution)/shard_map/all_to_all | solution.py:259
  233.3 13.4 %all-to-all-done = bf16[128,2,1024]{2,1,0:T(2,128)(2,1)S(1)} async-done(((bf16[128,2,1024]{2,1,0:T(2,128)(2,1)}), bf16[128,2,1024]{2,1,0:T(2,128)(2,1)S(1)}, u32[]{:S(2)}, u32[]{:S(2)}) %all-to-all-start) | async-done | bytes 524320 | tf_op jit(solution)/shard_map/all_to_all | solution.py:259
  248.6 1.2 fusion.61
  251.3 21.3 %all-gather.7.cloned.1.call-done = bf16[384,2048]{1,0:T(8,128)(2,1)} async-done(((bf16[96,2048]{1,0:T(8,128)(2,1)}), bf16[384,2048]{1,0:T(8,128)(2,1)}) %all-gather.7.cloned.1.call-update) | async-done | bytes 1572880 | tf_op jit(solution)/shard_map/all_gather | solution.py:136
  272.6 5.2 %fusion.111 = f32[384,704]{0,1:T(8,128)} fusion(bf16[384,2048]{1,0:T(8,128)(2,1)} %all-gather.7.cloned.1.call-done, bf16[2048,704]{1,0:T(8,128)(2,1)} %all-gather.9.cloned.1.call-done), kind=kOutput, calls=%fused_computation.264 | convolution fusion | flops 1107296256 | bytes 5537792 | tf_op jit(solution)/shard_map/dot_general | solution.py:142
  277.7 42.4 %all-gather.11.cloned.1.call-done = bf16[2048,704]{1,0:T(8,128)(2,1)} async-done(((bf16[64,704]{1,0:T(8,128)(2,1)}), bf16[2048,704]{1,0:T(8,128)(2,1)}) %all-gather.11.cloned.1.call-update) | async-done | bytes 2883600 | tf_op jit(solution)/shard_map/all_gather | solution.py:139
  320.2 46.3 %all-gather.13.cloned.1.call-done = bf16[2048,704]{1,0:T(8,128)(2,1)} async-done(((bf16[64,704]{1,0:T(8,128)(2,1)}), bf16[2048,704]{1,0:T(8,128)(2,1)}) %all-gather.13.cloned.1.call-update) | async-done | bytes 2883600 | tf_op jit(solution)/shard_map/all_gather | solution.py:140
  366.5 7.9 %fusion.62 = f32[384,2048]{1,0:T(8,128)} fusion(bf16[2048,704]{1,0:T(8,128)(2,1)} %all-gather.13.cloned.1.call-done, bf16[384,2048]{1,0:T(8,128)(2,1)S(1)} %copy-done.9, bf16[2048,704]{1,0:T(8,128)(2,1)} %all-gather.11.cloned.1.call-done, f32[384,704]{0,1:T(8,128)} %fusion.111), kind=kOutput, calls=%fused_computation.103 | convolution fusion | flops 2216214528 | bytes 11567104 | tf_op jit(solution)/shard_map/dot_general | solution.py:146
  374.7 37.1 %reduce-scatter.2.cloned.1.call-done = f32[96,2048]{1,0:T(8,128)} async-done(((f32[384,2048]{1,0:T(8,128)}), f32[96,2048]{1,0:T(8,128)}) %reduce-scatter.2.cloned.1.call-update) | async-done | bytes 786448 | tf_op jit(solution)/shard_map/reduce_scatter | solution.py:145
  411.8 1.2 convert_element_type.212
  414.0 1.0 reduce.13
  415.1 1.2 reshape.938
  416.2 8.0 %all-to-all-start.1 = ((bf16[128,2,1024]{2,1,0:T(2,128)(2,1)}), bf16[128,2,1024]{2,1,0:T(2,128)(2,1)S(1)}, u32[]{:S(2)}, u32[]{:S(2)}) async-start(bf16[128,2,1024]{2,1,0:T(2,128)(2,1)} %reshape.938), calls=%async_computation.2 | async-start | bytes 1048576 | tf_op jit(solution)/shard_map/all_to_all | solution.py:289
  424.3 13.5 %all-to-all-done.1 = bf16[128,2,1024]{2,1,0:T(2,128)(2,1)S(1)} async-done(((bf16[128,2,1024]{2,1,0:T(2,128)(2,1)}), bf16[128,2,1024]{2,1,0:T(2,128)(2,1)S(1)}, u32[]{:S(2)}, u32[]{:S(2)}) %all-to-all-start.1) | async-done | bytes 524320 | tf_op jit(solution)/shard_map/all_to_all | solution.py:289
  438.6 1.7 gather_fusion.3
  440.3 2.2 fusion.64
  (215 shorter events, 33.9 us)
Async XLA Ops:
  6.5 5.4 %copy-start = (bf16[2048,512]{1,0:T(8,128)(2,1)S(1)}, bf16[2048,512]{1,0:T(8,128)(2,1)}, u32[]{:S(2)}) copy-start(bf16[2048,512]{1,0:T(8,128)(2,1)} %param.29) | copy-start | bytes 6291460
  6.5 5.4 %copy-start.3 = (bf16[1,128,2048]{2,1,0:T(8,128)(2,1)S(1)}, bf16[1,128,2048]{2,1,0:T(8,128)(2,1)}, u32[]{:S(2)}) copy-start(bf16[1,128,2048]{2,1,0:T(8,128)(2,1)} %param.25) | copy-start | bytes 1572868
  6.5 140.9 %all-gather.15.cloned.1.call-start = ((), (), s32[]{:S(2)}) async-start(), calls=%async_computation.8 | async-start | bytes 34603008 | tf_op jit(solution)/shard_map/all_gather | solution.py:15
  8.6 3.8 copy-start.8
  11.9 6.1 %copy-start.6 = (s32[4,4]{1,0:T(4,128)S(1)}, s32[4,4]{1,0:T(4,128)}, u32[]{:S(2)}) copy-start(s32[4,4]{1,0:T(4,128)} %param.26) | copy-start | bytes 196
  11.9 6.6 %copy-start.4 = (bf16[4,2048]{1,0:T(4,128)(2,1)S(1)}, bf16[4,2048]{1,0:T(4,128)(2,1)}, u32[]{:S(2)}) copy-start(bf16[4,2048]{1,0:T(4,128)(2,1)} %param.35) | copy-start | bytes 49156
  11.9 6.7 %copy-start.10 = (bf16[2048,16]{0,1:T(8,128)(2,1)S(1)}, bf16[2048,16]{0,1:T(8,128)(2,1)}, u32[]{:S(2)}) copy-start(bf16[2048,16]{0,1:T(8,128)(2,1)} %param.32) | copy-start | bytes 196612
  12.5 6.5 %copy-start.11 = (bf16[16,512]{1,0:T(8,128)(2,1)S(1)}, bf16[16,512]{1,0:T(8,128)(2,1)}, u32[]{:S(2)}) copy-start(bf16[16,512]{1,0:T(8,128)(2,1)} %param.33) | copy-start | bytes 49156
  12.5 6.5 %copy-start.12 = (f32[512]{0:T(512)S(1)}, f32[512]{0:T(512)}, u32[]{:S(2)}) copy-start(f32[512]{0:T(512)} %param.34) | copy-start | bytes 6148
  13.1 6.8 %collective-permute-start = (bf16[3,2048]{1,0:T(4,128)(2,1)S(1)}, bf16[3,2048]{1,0:T(4,128)(2,1)S(1)}, u32[]{:S(2)}, u32[]{:S(2)}) collective-permute-start(bf16[3,2048]{1,0:T(4,128)(2,1)S(1)} %slice.105), channel_id=1, source_target_pairs={{0,1},{1,2},{2,3},{3,4},{4,5},{5,6},{6,7},{7,8},{8,9},{9,10},{10,1... | collective-permute-start | bytes 36872 | tf_op jit(solution)/shard_map/ppermute | solution.py:33
  21.2 40.4 %copy-start.7 = (bf16[512]{0:T(512)(128)(2,1)S(1)}, bf16[512]{0:T(512)(128)(2,1)}, u32[]{:S(2)}) copy-start(bf16[512]{0:T(512)(128)(2,1)} %param.36) | copy-start | bytes 3076
  21.2 41.3 %copy-start.5 = (bf16[2048]{0:T(1024)(128)(2,1)S(1)}, bf16[2048]{0:T(1024)(128)(2,1)}, u32[]{:S(2)}) copy-start(bf16[2048]{0:T(1024)(128)(2,1)} %param.38) | copy-start | bytes 12292
  30.4 1.0 copy-start.2
  31.5 219.8 %all-gather.9.cloned.1.call-start = ((), (), s32[]{:S(2)}) async-start(), calls=%async_computation.4 | async-start | bytes 3244032 | tf_op jit(solution)/shard_map/all_gather | solution.py:138
  226.0 20.7 %all-to-all-start = ((bf16[128,2,1024]{2,1,0:T(2,128)(2,1)}), bf16[128,2,1024]{2,1,0:T(2,128)(2,1)S(1)}, u32[]{:S(2)}, u32[]{:S(2)}) async-start(bf16[128,2,1024]{2,1,0:T(2,128)(2,1)} %reshape.936), calls=%async_computation | async-start | bytes 1048576 | tf_op jit(solution)/shard_map/all_to_all | solution.py:259
  233.2 39.4 %all-gather.7.cloned.1.call-start = ((), (), s32[]{:S(2)}) async-start(), calls=%async_computation.3 | async-start | bytes 1966080 | tf_op jit(solution)/shard_map/all_gather | solution.py:136
  249.8 70.3 %all-gather.11.cloned.1.call-start = ((), (), s32[]{:S(2)}) async-start(), calls=%async_computation.5 | async-start | bytes 3244032 | tf_op jit(solution)/shard_map/all_gather | solution.py:139
  250.4 116.1 %all-gather.13.cloned.1.call-start = ((), (), s32[]{:S(2)}) async-start(), calls=%async_computation.6 | async-start | bytes 3244032 | tf_op jit(solution)/shard_map/all_gather | solution.py:140
  251.0 160.7 %reduce-scatter.2.cloned.1.call-start = ((), (), s32[]{:S(2)}) async-start(), calls=%async_computation.7 | async-start | bytes 3932160 | tf_op jit(solution)/shard_map/reduce_scatter | solution.py:145
  272.6 93.9 %copy-start.9 = (bf16[384,2048]{1,0:T(8,128)(2,1)S(1)}, bf16[384,2048]{1,0:T(8,128)(2,1)}, u32[]{:S(2)}) copy-start(bf16[384,2048]{1,0:T(8,128)(2,1)} %all-gather.7.cloned.1.call-done) | copy-start | bytes 4718596
  416.2 21.6 %all-to-all-start.1 = ((bf16[128,2,1024]{2,1,0:T(2,128)(2,1)}), bf16[128,2,1024]{2,1,0:T(2,128)(2,1)S(1)}, u32[]{:S(2)}, u32[]{:S(2)}) async-start(bf16[128,2,1024]{2,1,0:T(2,128)(2,1)} %reshape.938), calls=%async_computation.2 | async-start | bytes 1048576 | tf_op jit(solution)/shard_map/all_to_all | solution.py:289
  438.6 4.0 copy-start.1
Sparse Core Ops, SparseCore 0:
  31.6 115.7 all-gather.14
  149.7 44.1 all-gather.8
  250.0 22.5 all-gather.6
  274.7 45.4 all-gather.10
  322.3 44.2 all-gather.12
  374.6 37.1 reduce-scatter.1
where the time goes:
time: 451 us; the launch traced here: 449 us
  waiting for transfers between devices  261 us (58%)
  other arithmetic  71.9 us (16%)
  matrix products  29.9 us (7%)
  blocking collectives  26.4 us (6%)
  starting transfers between devices  20.5 us (5%)
  local copies, waits for them, and re-layouts  19.7 us (4%)
  between operations  15.9 us (4%)
    all_gather x1, waiting for transfers between devices, prefix_2(): everything = jax.tree.map(lambda part: lax.all_gather(part, axis), shard)  84.9 us
    select_n x32, other arithmetic, lap(): return jax.tree.map(lambda a, b: jnp.where(reached, a, b), new, before)  47.7 us
    all_gather x1, waiting for transfers between devices, swiglu_rows(): lax.all_gather(down_weight, 'seq', axis=0, tiled=True)  46.3 us
    all_gather x1, waiting for transfers between devices, swiglu_rows(): lax.all_gather(w_up, 'seq', axis=0, tiled=True)  42.4 us
    reduce_scatter x1, waiting for transfers between devices, swiglu_rows(): lax.psum_scatter(lax.dot_general(hidden, down_full, (((1,), (1,)), ((), (...  37.1 us
    all_gather x1, blocking collectives, prefix_2(): everything = jax.tree.map(lambda part: lax.all_gather(part, axis), shard)  26.4 us
    all_gather x1, waiting for transfers between devices, swiglu_rows(): every_row = lax.all_gather(normed, 'req', axis=0, tiled=True)  21.3 us
    all_to_all x1, waiting for transfers between devices, shards(): lax.all_to_all(returning, ('req', 'seq'), split_axis=0, concat_axis=0, ti...  13.5 us
  transfers between devices with their start and end apart: 9, of which 7 were waited for; matrix products, arithmetic and copies ran while one was open for 20% of the time, Pallas kernels for 0%

commit v1 on v0

--- a/solution.py
+++ b/solution.py
@@ -133,7 +133,39 @@
     normed = rms_scale(resident.astype(jnp.float32), forward_norm_scale.astype(jnp.float32)).astype(
         jnp.bfloat16
     )
-    every_row = lax.all_gather(normed, "req", axis=0, tiled=True)
+
+    def assign_the_quotas(v0, bus_axis):
+        part_next, side_arr, step_out = (
+            lax.axis_size(bus_axis),
+            lax.axis_index(bus_axis),
+            v0.shape[0],
+        )
+        history = [idx * part_next if tick == 0 else idx for tick, idx in enumerate(v0.shape)]
+        h_now = top = v0
+        inter = lax.dynamic_update_slice_in_dim(
+            jnp.zeros(history, v0.dtype), v0, side_arr * step_out, axis=0
+        )
+        for s in [*range(1, part_next // 2 + 1)]:
+            h_now = lax.ppermute(
+                h_now,
+                axis_name=bus_axis,
+                perm=[(tick, (tick + 1) % part_next) for tick in range(part_next)],
+            )
+            inter = lax.dynamic_update_slice_in_dim(
+                inter, h_now, (side_arr - s) % part_next * step_out, axis=0
+            )
+            if 2 * s < part_next:
+                top = lax.ppermute(
+                    top,
+                    axis_name=bus_axis,
+                    perm=[(tick, (tick - 1) % part_next) for tick in range(part_next)],
+                )
+                inter = lax.dynamic_update_slice_in_dim(
+                    inter, top, (side_arr + s) % part_next * step_out, axis=0
+                )
+        return inter
+
+    every_row = assign_the_quotas(normed, "req")
     gate_full, up_full, down_full = (
         lax.all_gather(w_gate, "seq", axis=0, tiled=True),
         lax.all_gather(w_up, "seq", axis=0, tiled=True),

time: 451 us -> 376 us (0.83)
  waiting for transfers between devices: 261 us -> 184 us
    all_gather x1, waiting for transfers between devices: 46.3 us -> 0.01 us  [swiglu_rows(): lax.all_gather(down_weight, 'seq', axis=0, tiled=True)]
    all_gather x1, waiting for transfers between devices: 42.4 us -> 15 us  [swiglu_rows(): lax.all_gather(w_up, 'seq', axis=0, tiled=True)]
    all_gather x1 -> x0, waiting for transfers between devices: 21.3 us -> none  [swiglu_rows(): every_row = lax.all_gather(normed, 'req', axis=0, tiled=True)]
    ppermute x0 -> x3, waiting for transfers between devices: none -> 18.2 us  [the longest x2 18.2 us: assign_the_quotas(): lax.ppermute(h_now, axis_name=bus_axis, perm=[(tick, (tick + 1) % part_ne...]
  transfers between devices with their start and end apart: 9 -> 11, of which waited for: 7 -> 7; matrix products, arithmetic and copies ran while one was open for 20% -> 24% of each run, Pallas kernels for 0% -> 0%
where the time goes in v1:
time: 376 us; the launch traced here: 374 us
  waiting for transfers between devices  184 us (49%)
  other arithmetic  71.2 us (19%)
  matrix products  29.2 us (8%)
  blocking collectives  26.4 us (7%)
  starting transfers between devices  23 us (6%)
  local copies, waits for them, and re-layouts  21.1 us (6%)
  between operations  15.6 us (4%)
  loops' own time  4.02 us (1%)
    all_gather x1, waiting for transfers between devices, prefix_2(): everything = jax.tree.map(lambda part: lax.all_gather(part, axis), shard)  83.6 us
    select_n x32, other arithmetic, lap(): return jax.tree.map(lambda a, b: jnp.where(reached, a, b), new, before)  47.7 us
    reduce_scatter x1, waiting for transfers between devices, swiglu_rows(): lax.psum_scatter(lax.dot_general(hidden, down_full, (((1,), (1,)), ((), (...  37.1 us
    all_gather x1, blocking collectives, prefix_2(): everything = jax.tree.map(lambda part: lax.all_gather(part, axis), shard)  26.4 us
    ppermute x2, waiting for transfers between devices, assign_the_quotas(): lax.ppermute(h_now, axis_name=bus_axis, perm=[(tick, (tick + 1) % part_ne...  18.2 us
    all_gather x1, waiting for transfers between devices, swiglu_rows(): lax.all_gather(w_up, 'seq', axis=0, tiled=True)  15 us
    all_to_all x1, waiting for transfers between devices, shards(): lax.all_to_all(outgoing, ('req', 'seq'), split_axis=0, concat_axis=0, til...  14.5 us
    all_to_all x1, waiting for transfers between devices, shards(): lax.all_to_all(returning, ('req', 'seq'), split_axis=0, concat_axis=0, ti...  13.5 us
  transfers between devices with their start and end apart: 11, of which 7 were waited for; matrix products, arithmetic and copies ran while one was open for 24% of the time, Pallas kernels for 0%

profile of v1, /device:TPU:1, one launch (start us, length us, event | category | flops | bytes accessed | tf_op | source)
XLA Modules:
  0.0 374.3 jit_solution(17466149721229861402)
XLA Ops:
  7.4 1.2 fusion.55
  8.6 3.2 convolution_convert_fusion
  12.3 1.1 copy-done.8
  14.0 4.9 %collective-permute-start = (bf16[3,2048]{1,0:T(4,128)(2,1)S(1)}, bf16[3,2048]{1,0:T(4,128)(2,1)S(1)}, u32[]{:S(2)}, u32[]{:S(2)}) collective-permute-start(bf16[3,2048]{1,0:T(4,128)(2,1)S(1)} %slice.105), channel_id=1, source_target_pairs={{0,1},{1,2},{2,3},{3,4},{4,5},{5,6},{6,7},{7,8},{8,9},{9,10},{10,1... | collective-permute-start | bytes 36872 | tf_op jit(solution)/shard_map/ppermute | solution.py:33
  22.1 9.0 %while.38 = (s32[]{:T(128)}, f32[2,256,512]{2,1,0:T(8,128)S(1)}, f32[2,64,2,256]{3,2,1,0:T(2,128)S(1)}, s32[2,64]{1,0:T(2,128)S(1)}, s32[2]{0:T(128)S(1)}, /*ind...) while((s32[]{:T(128)}, f32[2,256,512]{2,1,0:T(8,128)S(1)}, ...), condition=%wide.region_8.9_spmd.clone, body=%wide.region_7.8_spmd.clone.sunk | while | flops 227418752 | bytes 3230365 | solution.py:265
  37.2 26.4 %all_gather.19 = f32[32,2,256]{2,1,0:T(2,128)S(1)} all-gather(f32[1,2,256]{2,1,0:T(2,128)S(1)} %mul.407), channel_id=1, replica_groups=mesh['req'=4,'seq'=32] {'seq'}, dimensions={0}, use_global_device_ids=true | all-gather | bytes 67584 | tf_op jit(solution)/shard_map/all_gather | solution.py:15
  64.5 83.6 %all-gather.12.cloned.1.call-done = f32[64,256,512]{2,1,0:T(8,128)} async-done(((f32[2,256,512]{2,1,0:T(8,128)}), f32[64,256,512]{2,1,0:T(8,128)}) %all-gather.12.cloned.1.call-update) | async-done | bytes 33554448 | tf_op jit(solution)/shard_map/all_gather | solution.py:15
  148.2 49.0 %while.39 = (s32[]{:T(128)}, f32[2,256,512]{2,1,0:T(8,128)S(1)}, s32[]{:T(128)}, f32[32,2,256]{2,1,0:T(2,128)S(1)}, f32[32,2,256,512]{3,2,1,0:T(8,128)}, /*index=5*/s32[]{:T(128)}, s32[]{:T(128)}) while((s32[]{:T(128)}, f32[2,256,512]{2,1,0:T(8,128)S(1)}, s32[]{:T(128)}, f32[32,2,256]{2,1,0:T(2,128)S(1)}, ...), condition=%wide.region_10.11_spmd.clone, body=%wide.region_9.10_spmd.clone.sunk | while | flops 1048580 | bytes 3151977 | solution.py:27
  148.2 1.5 fusion.167
  149.7 1.5 fusion.167
  151.2 1.5 fusion.167
  152.8 1.5 fusion.167
  154.3 1.5 fusion.167
  155.8 1.5 fusion.167
  157.3 1.5 fusion.167
  158.9 1.5 fusion.167
  160.4 1.5 fusion.167
  161.9 1.5 fusion.167
  163.5 1.5 fusion.167
  165.0 1.5 fusion.167
  166.5 1.5 fusion.167
  168.1 1.5 fusion.167
  169.6 1.5 fusion.167
  171.1 1.5 fusion.167
  172.6 1.5 fusion.167
  174.2 1.5 fusion.167
  175.7 1.5 fusion.167
  177.2 1.5 fusion.167
  178.7 1.5 fusion.167
  180.3 1.5 fusion.167
  181.9 1.5 fusion.167
  183.4 1.5 fusion.167
  184.9 1.5 fusion.167
  186.5 1.5 fusion.167
  188.0 1.5 fusion.167
  189.6 1.5 fusion.167
  191.1 1.5 fusion.167
  192.6 1.5 fusion.167
  194.2 1.5 fusion.167
  195.7 1.5 fusion.167
  197.2 19.7 %while.37 = (s32[]{:T(128)}, f32[2,256,512]{2,1,0:T(8,128)S(1)}, f32[2,64,2,512]{3,1,2,0:T(8,128)S(1)}, f32[2,64,2,256]{3,2,1,0:T(2,128)S(1)}, s32[2,64]{1,0:T(2...) while((s32[]{:T(128)}, f32[2,256,512]{2,1,0:T(8,128)S(1)}, ...), condition=%wide.region_13.14_spmd, body=%wide.region_11.13_spmd.sunk | while | flops 447611648 | bytes 7385501 | solution.py:267
  199.3 3.0 multiply_reduce_fusion.3
  206.0 1.0 convolution_add_fusion.6
  209.2 3.0 multiply_reduce_fusion.3
  215.9 1.0 convolution_add_fusion.6
  218.0 4.9 %fusion.53 = bf16[128,2048]{1,0:T(8,128)(2,1)S(1)} fusion(bf16[1024,2048]{1,0:T(8,128)(2,1)} %param.37, bf16[1,128,2048]{2,1,0:T(8,128)(2,1)S(1)} %copy-done.3, f32[128,1024]{1,0:T(8,128)S(1)} %bitcast.254, f32[128,1024]{1,0:T(8,128)S(1)} %bitcast.253, f32[1024]{0:T(1024)S(1)} %bitcast.261, bf16[2048,1024]{1,0:T(8,128)(2,1)} %param.31, ...), kind=kOutput, calls=%fused_computation.82 | convolution fusion | flops 1076625408 | bytes 10498560 | tf_op jit(solution)/shard_map/dot_general | solution.py:273
  224.6 1.0 reduce.12
  225.6 1.2 reshape.936
  226.8 7.1 %all-to-all-start = ((bf16[128,2,1024]{2,1,0:T(2,128)(2,1)}), bf16[128,2,1024]{2,1,0:T(2,128)(2,1)S(1)}, u32[]{:S(2)}, u32[]{:S(2)}) async-start(bf16[128,2,1024]{2,1,0:T(2,128)(2,1)} %reshape.936), calls=%async_computation | async-start | bytes 1048576 | tf_op jit(solution)/shard_map/all_to_all | solution.py:291
  234.1 14.5 %all-to-all-done = bf16[128,2,1024]{2,1,0:T(2,128)(2,1)S(1)} async-done(((bf16[128,2,1024]{2,1,0:T(2,128)(2,1)}), bf16[128,2,1024]{2,1,0:T(2,128)(2,1)S(1)}, u32[]{:S(2)}, u32[]{:S(2)}) %all-to-all-start) | async-done | bytes 524320 | tf_op jit(solution)/shard_map/all_to_all | solution.py:291
  251.5 2.4 collective-permute-start.2
  253.8 8.2 %collective-permute-done.1 = bf16[96,2048]{1,0:T(8,128)(2,1)S(1)} collective-permute-done((bf16[96,2048]{1,0:T(8,128)(2,1)S(1)}, bf16[96,2048]{1,0:T(8,128)(2,1)S(1)}, u32[]{:S(2)}, u32[]{:S(2)}) %collective-permute-start.1) | collective-permute-done | bytes 393248 | tf_op jit(solution)/shard_map/ppermute | solution.py:149
  262.2 10.0 %collective-permute-done.3 = bf16[96,2048]{1,0:T(8,128)(2,1)S(1)} collective-permute-done((bf16[96,2048]{1,0:T(8,128)(2,1)S(1)}, bf16[96,2048]{1,0:T(8,128)(2,1)S(1)}, u32[]{:S(2)}, u32[]{:S(2)}) %collective-permute-start.3) | collective-permute-done | bytes 393248 | tf_op jit(solution)/shard_map/ppermute | solution.py:149
  272.2 4.6 %fusion.113 = f32[384,704]{0,1:T(8,128)} fusion(bf16[384,2048]{1,0:T(8,128)(2,1)S(1)} %constant_dynamic-update-slice_fusion, bf16[2048,704]{1,0:T(8,128)(2,1)} %all-gather.6.cloned.1.call-done), kind=kOutput, calls=%fused_computation.268 | convolution fusion | flops 1107296256 | bytes 5537792 | tf_op jit(solution)/shard_map/dot_general | solution.py:174
  276.8 15.0 %all-gather.8.cloned.1.call-done = bf16[2048,704]{1,0:T(8,128)(2,1)} async-done(((bf16[64,704]{1,0:T(8,128)(2,1)}), bf16[2048,704]{1,0:T(8,128)(2,1)}) %all-gather.8.cloned.1.call-update) | async-done | bytes 2883600 | tf_op jit(solution)/shard_map/all_gather | solution.py:171
  291.8 7.9 %fusion.61 = f32[384,2048]{1,0:T(8,128)} fusion(bf16[2048,704]{1,0:T(8,128)(2,1)} %all-gather.10.cloned.1.call-done, f32[384,704]{0,1:T(8,128)} %fusion.113, bf16[384,2048]{1,0:T(8,128)(2,1)S(1)} %constant_dynamic-update-slice_fusion, bf16[2048,704]{1,0:T(8,128)(2,1)} %all-gather.8.cloned.1.call-done), kind=kOutput, calls=%fused_computation.103 | convolution fusion | flops 2216214528 | bytes 11567104 | tf_op jit(solution)/shard_map/dot_general | solution.py:178
  299.9 37.1 %reduce-scatter.2.cloned.1.call-done = f32[96,2048]{1,0:T(8,128)} async-done(((f32[384,2048]{1,0:T(8,128)}), f32[96,2048]{1,0:T(8,128)}) %reduce-scatter.2.cloned.1.call-update) | async-done | bytes 786448 | tf_op jit(solution)/shard_map/reduce_scatter | solution.py:177
  337.0 1.2 convert_element_type.212
  339.3 1.0 reduce.13
  340.3 1.2 reshape.938
  341.5 8.0 %all-to-all-start.1 = ((bf16[128,2,1024]{2,1,0:T(2,128)(2,1)}), bf16[128,2,1024]{2,1,0:T(2,128)(2,1)S(1)}, u32[]{:S(2)}, u32[]{:S(2)}) async-start(bf16[128,2,1024]{2,1,0:T(2,128)(2,1)} %reshape.938), calls=%async_computation.2 | async-start | bytes 1048576 | tf_op jit(solution)/shard_map/all_to_all | solution.py:321
  349.6 13.5 %all-to-all-done.1 = bf16[128,2,1024]{2,1,0:T(2,128)(2,1)S(1)} async-done(((bf16[128,2,1024]{2,1,0:T(2,128)(2,1)}), bf16[128,2,1024]{2,1,0:T(2,128)(2,1)S(1)}, u32[]{:S(2)}, u32[]{:S(2)}) %all-to-all-start.1) | async-done | bytes 524320 | tf_op jit(solution)/shard_map/all_to_all | solution.py:321
  363.8 1.7 gather_fusion.3
  365.6 2.2 fusion.63
  (219 shorter events, 35.9 us)
Async XLA Ops:
  6.5 5.3 %copy-start = (bf16[2048,512]{1,0:T(8,128)(2,1)S(1)}, bf16[2048,512]{1,0:T(8,128)(2,1)}, u32[]{:S(2)}) copy-start(bf16[2048,512]{1,0:T(8,128)(2,1)} %param.29) | copy-start | bytes 6291460
  6.5 141.6 %all-gather.12.cloned.1.call-start = ((), (), s32[]{:S(2)}) async-start(), calls=%async_computation.7 | async-start | bytes 34603008 | tf_op jit(solution)/shard_map/all_gather | solution.py:15
  8.6 3.2 copy-start.3
  11.8 1.6 copy-start.8
  13.4 5.6 %copy-start.6 = (s32[4,4]{1,0:T(4,128)S(1)}, s32[4,4]{1,0:T(4,128)}, u32[]{:S(2)}) copy-start(s32[4,4]{1,0:T(4,128)} %param.26) | copy-start | bytes 196
  13.4 6.0 %copy-start.4 = (bf16[4,2048]{1,0:T(4,128)(2,1)S(1)}, bf16[4,2048]{1,0:T(4,128)(2,1)}, u32[]{:S(2)}) copy-start(bf16[4,2048]{1,0:T(4,128)(2,1)} %param.35) | copy-start | bytes 49156
  13.4 6.1 %copy-start.9 = (bf16[2048,16]{0,1:T(8,128)(2,1)S(1)}, bf16[2048,16]{0,1:T(8,128)(2,1)}, u32[]{:S(2)}) copy-start(bf16[2048,16]{0,1:T(8,128)(2,1)} %param.32) | copy-start | bytes 196612
  13.4 6.4 %copy-start.10 = (bf16[16,512]{1,0:T(8,128)(2,1)S(1)}, bf16[16,512]{1,0:T(8,128)(2,1)}, u32[]{:S(2)}) copy-start(bf16[16,512]{1,0:T(8,128)(2,1)} %param.33) | copy-start | bytes 49156
  13.4 6.4 %copy-start.11 = (f32[512]{0:T(512)S(1)}, f32[512]{0:T(512)}, u32[]{:S(2)}) copy-start(f32[512]{0:T(512)} %param.34) | copy-start | bytes 6148
  14.0 6.8 %collective-permute-start = (bf16[3,2048]{1,0:T(4,128)(2,1)S(1)}, bf16[3,2048]{1,0:T(4,128)(2,1)S(1)}, u32[]{:S(2)}, u32[]{:S(2)}) collective-permute-start(bf16[3,2048]{1,0:T(4,128)(2,1)S(1)} %slice.105), channel_id=1, source_target_pairs={{0,1},{1,2},{2,3},{3,4},{4,5},{5,6},{6,7},{7,8},{8,9},{9,10},{10,1... | collective-permute-start | bytes 36872 | tf_op jit(solution)/shard_map/ppermute | solution.py:33
  22.1 41.6 %copy-start.7 = (bf16[512]{0:T(512)(128)(2,1)S(1)}, bf16[512]{0:T(512)(128)(2,1)}, u32[]{:S(2)}) copy-start(bf16[512]{0:T(512)(128)(2,1)} %param.36) | copy-start | bytes 3076
  22.1 42.4 %copy-start.5 = (bf16[2048]{0:T(1024)(128)(2,1)S(1)}, bf16[2048]{0:T(1024)(128)(2,1)}, u32[]{:S(2)}) copy-start(bf16[2048]{0:T(1024)(128)(2,1)} %param.38) | copy-start | bytes 12292
  31.2 1.0 copy-start.2
  32.2 240.0 %all-gather.6.cloned.1.call-start = ((), (), s32[]{:S(2)}) async-start(), calls=%async_computation.3 | async-start | bytes 3244032 | tf_op jit(solution)/shard_map/all_gather | solution.py:170
  33.0 243.8 %all-gather.10.cloned.1.call-start = ((), (), s32[]{:S(2)}) async-start(), calls=%async_computation.5 | async-start | bytes 3244032 | tf_op jit(solution)/shard_map/all_gather | solution.py:172
  33.7 258.1 %all-gather.8.cloned.1.call-start = ((), (), s32[]{:S(2)}) async-start(), calls=%async_computation.4 | async-start | bytes 3244032 | tf_op jit(solution)/shard_map/all_gather | solution.py:171
  226.8 21.7 %all-to-all-start = ((bf16[128,2,1024]{2,1,0:T(2,128)(2,1)}), bf16[128,2,1024]{2,1,0:T(2,128)(2,1)S(1)}, u32[]{:S(2)}, u32[]{:S(2)}) async-start(bf16[128,2,1024]{2,1,0:T(2,128)(2,1)} %reshape.936), calls=%async_computation | async-start | bytes 1048576 | tf_op jit(solution)/shard_map/all_to_all | solution.py:291
  233.9 103.1 %reduce-scatter.2.cloned.1.call-start = ((), (), s32[]{:S(2)}) async-start(), calls=%async_computation.6 | async-start | bytes 3932160 | tf_op jit(solution)/shard_map/reduce_scatter | solution.py:177
  251.1 11.0 %collective-permute-start.1 = (bf16[96,2048]{1,0:T(8,128)(2,1)S(1)}, bf16[96,2048]{1,0:T(8,128)(2,1)S(1)}, u32[]{:S(2)}, u32[]{:S(2)}) collective-permute-start(bf16[96,2048]{1,0:T(8,128)(2,1)S(1)} %get-tuple-element.358), channel_id=1, source_target_pairs={{0,32},{32,64},{64,96},{96,0},{1,33},{33,65},{65,97},{97,1},{2,34}... | collective-permute-start | bytes 1179656 | tf_op jit(solution)/shard_map/ppermute | solution.py:149
  251.5 10.7 %collective-permute-start.2 = (bf16[96,2048]{1,0:T(8,128)(2,1)S(1)}, bf16[96,2048]{1,0:T(8,128)(2,1)S(1)}, u32[]{:S(2)}, u32[]{:S(2)}) collective-permute-start(bf16[96,2048]{1,0:T(8,128)(2,1)S(1)} %get-tuple-element.358), channel_id=1, source_target_pairs={{0,96},{32,0},{64,32},{96,64},{1,97},{33,1},{65,33},{97,65},{2,98}... | collective-permute-start | bytes 1179656 | tf_op jit(solution)/shard_map/ppermute | solution.py:158
  262.1 10.1 %collective-permute-start.3 = (bf16[96,2048]{1,0:T(8,128)(2,1)S(1)}, bf16[96,2048]{1,0:T(8,128)(2,1)S(1)}, u32[]{:S(2)}, u32[]{:S(2)}) collective-permute-start(bf16[96,2048]{1,0:T(8,128)(2,1)S(1)} %collective-permute-done.1), channel_id=1, source_target_pairs={{0,32},{32,64},{64,96},{96,0},{1,33},{33,65},{65,97},{97,1},{2,34}... | collective-permute-start | bytes 1179656 | tf_op jit(solution)/shard_map/ppermute | solution.py:149
  341.5 21.6 %all-to-all-start.1 = ((bf16[128,2,1024]{2,1,0:T(2,128)(2,1)}), bf16[128,2,1024]{2,1,0:T(2,128)(2,1)S(1)}, u32[]{:S(2)}, u32[]{:S(2)}) async-start(bf16[128,2,1024]{2,1,0:T(2,128)(2,1)} %reshape.938), calls=%async_computation.2 | async-start | bytes 1048576 | tf_op jit(solution)/shard_map/all_to_all | solution.py:321
  363.8 4.0 %copy-start.1 = (bf16[2048,512]{1,0:T(8,128)(2,1)S(1)}, bf16[2048,512]{1,0:T(8,128)(2,1)}, u32[]{:S(2)}) copy-start(bf16[2048,512]{1,0:T(8,128)(2,1)} %param.29) | copy-start | bytes 6291460
Sparse Core Ops, SparseCore 0:
  32.3 115.7 all-gather.11
  150.4 44.1 all-gather.5
  196.8 47.6 all-gather.9
  246.7 45.0 all-gather.7
  299.8 37.1 reduce-scatter.1
